TPU v7x, 256 devices: a whole 4x4x8 slice. The times are simulated.
256 devices in a mesh: tensor: 8 (over x, core), req: 32 (over y, z).
Axes of the slice: x: 4, y: 4, z: 8, core: 2. Of those that a mesh axis runs over, the one named last changes fastest.
Arguments:
- attention_output: bfloat16 [16384, 4096], P('req', 'tensor'), may hold values from -6 to 6
- residual: bfloat16 [16384, 8192], P('req', 'tensor'), may hold values from -6 to 6
- projection_weight: bfloat16 [4096, 8192], P('tensor'), may hold values from -0.09375 to 0.09375
- adapter_down_maps: bfloat16 [256, 4096, 64], P('req', 'tensor'), may hold values from -0.09375 to 0.09375
- adapter_up_maps: bfloat16 [256, 64, 8192], P('req', None, 'tensor'), may hold values from -0.75 to 0.75
- adapter_pool_slot: int32 [256], replicated, may hold values from 0 to 255, as said below
- request_adapter_id: int32 [32, 32], replicated, may hold values from 0 to 255, as said below
- request_token_length: int32 [32, 32], P('req'), may hold values from 1 to 32, 512 in all within a row
Outputs:
- mixed: bfloat16 [16384, 8192], P('req', 'tensor')
Inputs may be any that keep to these rules, and one draw needn't show every extreme that they name: `adapter_pool_slot`: each slot appears once; the slot s lies on index s // 8 of req, its owner. `request_adapter_id`: the 32 requests of one group use adapters with 32 distinct owners. `request_token_length`: each group's lengths sum to 512; in each group the largest is exactly 32.
All inputs are finite; a program needn't handle non-finite values.
Results may differ from a plain program's by a relative error of at most 0.014.
Values may be sent and summed in bfloat16 or wider, within the bound.
No kernel may reach another device: no remote copies, remote signals or barrier semaphores. Data moves between devices by JAX's collectives and lax.ppermute only.
A program may use at most 128 MiB of HBM per device.

v0:
```python
import jax
import jax.numpy as jnp
from jax import lax
from jax.sharding import PartitionSpec as P


def per_device(
    attention_output,
    residual,
    projection_weight,
    adapter_down_maps,
    adapter_up_maps,
    adapter_pool_slot,
    request_adapter_id,
    request_token_length,
):
    groups = lax.axis_size("req")
    me_index = lax.axis_index("req")
    tok_rows = attention_output.shape[0]
    features = attention_output.shape[1]
    pooled_adapter_rows = adapter_down_maps.shape[0]
    lengths = request_token_length[0]
    requests = lengths.shape[0]
    ends = jnp.cumsum(lengths)
    starts = ends - lengths
    my_ids = lax.dynamic_index_in_dim(request_adapter_id, me_index, 0, keepdims=False)
    my_owner = jnp.take(adapter_pool_slot, my_ids) // pooled_adapter_rows
    positions = jnp.arange(tok_rows, dtype=jnp.int32)
    tok_req = jnp.sum((positions[:, None] >= ends[None, :]).astype(jnp.int32), 1)
    req_hot = tok_req[:, None] == jnp.arange(requests, dtype=jnp.int32)[None, :]
    tok_owner = jnp.sum(jnp.where(req_hot, my_owner[None, :], 0), 1)
    tok_start = jnp.sum(jnp.where(req_hot, starts[None, :], 0), 1)
    all_slots = jnp.take(adapter_pool_slot, request_adapter_id)
    mine = all_slots // pooled_adapter_rows == me_index
    block_row_index = jnp.sum(jnp.where(mine, all_slots % pooled_adapter_rows, 0), 1)
    selected_down_map = jnp.take(adapter_down_maps, block_row_index, axis=0)
    selected_up_map = jnp.take(adapter_up_maps, block_row_index, axis=0)
    most_rows = 2 * tok_rows // requests
    owner_hot = my_owner[None, :] == jnp.arange(groups, dtype=jnp.int32)[:, None]
    first = jnp.sum(jnp.where(owner_hot, starts[None, :], 0), 1)
    count = jnp.sum(jnp.where(owner_hot, lengths[None, :], 0), 1)
    slot_pos = jnp.arange(most_rows, dtype=jnp.int32)
    source = first[:, None] + slot_pos[None, :]
    valid = slot_pos[None, :] < count[:, None]
    padded = jnp.concatenate([attention_output, jnp.zeros((1, features), jnp.bfloat16)], 0)
    outgoing = jnp.take(padded, jnp.where(valid, source, tok_rows), axis=0)
    partial_value = jnp.dot(attention_output, projection_weight, preferred_element_type=jnp.float32)
    base = lax.psum_scatter(
        partial_value.astype(jnp.bfloat16), "tensor", scatter_dimension=1, tiled=True
    ).astype(jnp.float32)
    reduced_rows = jnp.einsum(
        "sdy,syj->sdj",
        lax.all_to_all(outgoing, "req", split_axis=0, concat_axis=0, tiled=True),
        selected_down_map,
        preferred_element_type=jnp.float32,
    )
    reduced_rows = lax.psum(reduced_rows.astype(jnp.bfloat16), "tensor").astype(jnp.float32)
    raised_output = jnp.einsum(
        "iut,itb->iub",
        reduced_rows.astype(jnp.bfloat16),
        selected_up_map,
        preferred_element_type=jnp.float32,
    )
    returned = lax.all_to_all(
        raised_output.astype(jnp.bfloat16), "req", split_axis=0, concat_axis=0, tiled=True
    ).astype(raised_output.dtype)
    flat = returned.reshape(groups * most_rows, returned.shape[2])
    delta = jnp.take(flat, tok_owner * most_rows + positions - tok_start, axis=0)
    return (residual.astype(jnp.float32) + base + delta).astype(jnp.bfloat16)


def solution(mesh):
    in_specs = (
        P("req", "tensor"),
        P("req", "tensor"),
        P("tensor", None),
        P("req", "tensor", None),
        P("req", None, "tensor"),
        P(),
        P(),
        P("req", None),
    )
    out_specs = P("req", "tensor")
    return jax.shard_map(
        per_device, mesh=mesh, in_specs=in_specs, out_specs=out_specs, check_vma=False
    )
```

profile of v0, /device:TPU:6, one launch (start us, length us, event | category | flops | bytes accessed | tf_op | source)
XLA Modules:
  0.0 203.0 jit_solution(16693608785722491008)
XLA Ops:
  6.5 0.8 fusion.22
  7.3 0.7 copy.11
  8.1 0.1 reduce
  8.2 1.4 gather_fusion
  9.6 0.7 fusion.24
  10.3 0.8 select_reduce_fusion.3
  11.4 1.1 concatenate.3
  12.5 4.0 %gather_fusion.1 = bf16[1024,512]{1,0:T(8,128)(2,1)S(1)} fusion(bf16[513,512]{1,0:T(8,128)(2,1)S(1)} %concatenate.3, s32[1024]{0:T(1024)S(1)} %broadcast_clamp_fusion), kind=kCustom, calls=%fused_computation.1 | custom fusion | bytes 2101248 | tf_op jit(solution)/shard_map/jit(_take)/gather | solution.py:46
  16.5 1.2 broadcast_select_fusion
  17.6 11.5 %all-to-all-start = ((bf16[32,32,512]{2,1,0:T(8,128)(2,1)}), bf16[32,32,512]{2,1,0:T(8,128)(2,1)S(1)}, u32[]{:S(2)}, u32[]{:S(2)}) async-start(bf16[32,32,512]{2,1,0:T(8,128)(2,1)} %broadcast_select_fusion), calls=%async_computation.1 | async-start | bytes 2097152 | tf_op jit(solution)/shard_map/all_to_all | solution.py:53
  29.3 6.8 %gather_fusion.2 = s32[1024]{0:T(1024)S(1)} fusion(s32[256]{0:T(256)S(1)} %copy-done.1, s32[1024]{0:T(1024)S(1)} %broadcast_clamp_fusion.1), kind=kCustom, calls=%fused_computation.2 | custom fusion | bytes 12288 | tf_op jit(solution)/shard_map/jit(_take)/gather | solution.py:33
  36.2 0.1 fusion.16
  36.4 2.0 %gather_fusion.3 = bf16[32,512,64]{1,2,0:T(8,128)(2,1)} fusion(bf16[8,512,64]{1,2,0:T(8,128)(2,1)S(1)} %copy-done.2, s32[1024]{0:T(1024)S(1)} %pad_clamp_fusion.1), kind=kCustom, calls=%fused_computation.3 | custom fusion | bytes 4194432 | tf_op jit(solution)/shard_map/jit(_take)/gather | solution.py:36
  38.4 19.3 %all-to-all-done = bf16[32,32,512]{2,1,0:T(8,128)(2,1)S(1)} async-done(((bf16[32,32,512]{2,1,0:T(8,128)(2,1)}), bf16[32,32,512]{2,1,0:T(8,128)(2,1)S(1)}, u32[]{:S(2)}, u32[]{:S(2)}) %all-to-all-start) | async-done | bytes 1048608 | tf_op jit(solution)/shard_map/all_to_all | solution.py:53
  57.7 3.1 %fusion.10 = bf16[32,32,64]{2,1,0:T(8,128)(2,1)} fusion(bf16[32,32,512]{2,1,0:T(8,128)(2,1)S(1)} %all-to-all-done, bf16[32,512,64]{1,2,0:T(8,128)(2,1)} %gather_fusion.3, pred[32]{0:T(512)(128)(4,1)S(1)} %compare_and_fusion), kind=kOutput, calls=%fused_computation.17 | convolution fusion | flops 68222976 | bytes 3276832 | tf_op jit(solution)/shard_map/sdy,syj->sdj/dot_general | solution.py:51
  60.9 10.1 %convolution_convert_fusion = bf16[512,8192]{1,0:T(8,128)(2,1)} fusion(bf16[512,512]{1,0:T(8,128)(2,1)S(1)} %copy-done.3, bf16[512,8192]{1,0:T(8,128)(2,1)} %param.10), kind=kOutput, calls=%fused_computation.6 | convolution fusion | flops 4299161600 | bytes 17301504 | tf_op jit(solution)/shard_map/dot_general | solution.py:47
  71.0 2.8 %gather_fusion.4 = bf16[32,64,1024]{2,1,0:T(8,128)(2,1)} fusion(bf16[8,64,1024]{2,1,0:T(8,128)(2,1)S(1)} %copy-done, s32[1024]{0:T(1024)S(1)} %pad_clamp_fusion.1), kind=kCustom, calls=%fused_computation.4 | custom fusion | bytes 8388736 | tf_op jit(solution)/shard_map/jit(_take)/gather | solution.py:37
  73.8 46.8 %all-reduce.3.cloned.1.call-done = bf16[32,32,64]{2,1,0:T(8,128)(2,1)} async-done(((bf16[32,32,64]{2,1,0:T(8,128)(2,1)}), bf16[32,32,64]{2,1,0:T(8,128)(2,1)}) %all-reduce.3.cloned.1.call-update) | async-done | bytes 131088 | tf_op jit(solution)/shard_map/psum | solution.py:57
  120.6 4.4 %fusion.7 = bf16[32,32,1024]{2,1,0:T(8,128)(2,1)} fusion(bf16[32,32,64]{2,1,0:T(8,128)(2,1)} %all-reduce.3.cloned.1.call-done, bf16[32,64,1024]{2,1,0:T(8,128)(2,1)} %gather_fusion.4, pred[32]{0:T(512)(128)(4,1)S(1)} %compare_and_fusion), kind=kOutput, calls=%fused_computation.16 | convolution fusion | flops 137363456 | bytes 6422560 | tf_op jit(solution)/shard_map/iut,itb->iub/dot_general | solution.py:58
  125.1 9.8 %all-to-all-start.1 = ((bf16[32,32,1024]{2,1,0:T(8,128)(2,1)}), bf16[32,32,1024]{2,1,0:T(8,128)(2,1)S(1)}, u32[]{:S(2)}, u32[]{:S(2)}) async-start(bf16[32,32,1024]{2,1,0:T(8,128)(2,1)} %fusion.7), calls=%async_computation.2 | async-start | bytes 4194304 | tf_op jit(solution)/shard_map/all_to_all | solution.py:64
  135.2 50.4 %all-to-all-done.1 = bf16[32,32,1024]{2,1,0:T(8,128)(2,1)S(1)} async-done(((bf16[32,32,1024]{2,1,0:T(8,128)(2,1)}), bf16[32,32,1024]{2,1,0:T(8,128)(2,1)S(1)}, u32[]{:S(2)}, u32[]{:S(2)}) %all-to-all-start.1) | async-done | bytes 2097184 | tf_op jit(solution)/shard_map/all_to_all | solution.py:64
  185.6 2.6 %bitcast_convert_fusion = f32[1024,1024]{1,0:T(8,128)} fusion(bf16[32,32,1024]{2,1,0:T(8,128)(2,1)S(1)} %all-to-all-done.1), kind=kLoop, calls=%fused_computation.10 | loop fusion | flops 1048576 | bytes 6291456 | tf_op jit(solution)/shard_map/reshape | solution.py:67
  188.2 5.0 %gather_fusion.5 = f32[512,1024]{1,0:T(8,128)S(1)} fusion(f32[1024,1024]{1,0:T(8,128)} %bitcast_convert_fusion, s32[1024]{0:T(1024)S(1)} %pad_clamp_fusion), kind=kCustom, calls=%fused_computation.5 | custom fusion | bytes 4196352 | tf_op jit(solution)/shard_map/jit(_take)/gather | solution.py:68
  193.2 2.9 %add_convert_fusion = bf16[512,1024]{1,0:T(8,128)(2,1)} fusion(f32[512,1024]{1,0:T(8,128)S(1)} %gather_fusion.5, bf16[512,1024]{1,0:T(8,128)(2,1)} %reduce-scatter.2.cloned.1.call-done, bf16[512,1024]{1,0:T(8,128)(2,1)} %param.9, pred[512]{0:T(512)(128)(4,1)S(1)} %compare_and_fusion.1), kind=kLoop, calls=%fused_computation.11 | loop fusion | flops 3145728 | bytes 5243392 | tf_op jit(solution)/shard_map/convert_element_type | solution.py:69
  (34 shorter events, 0.9 us)
Async XLA Ops:
  6.5 64.5 %copy-start = (bf16[8,64,1024]{2,1,0:T(8,128)(2,1)S(1)}, bf16[8,64,1024]{2,1,0:T(8,128)(2,1)}, u32[]{:S(2)}) copy-start(bf16[8,64,1024]{2,1,0:T(8,128)(2,1)} %param.12) | copy-start | bytes 3145732
  16.4 12.7 %copy-start.4 = (s32[32,32]{1,0:T(8,128)S(1)}, s32[32,32]{1,0:T(8,128)}, u32[]{:S(2)}) copy-start(s32[32,32]{1,0:T(8,128)} %param.14) | copy-start | bytes 12292
  16.4 12.8 %copy-start.1 = (s32[256]{0:T(256)S(1)}, s32[256]{0:T(256)}, u32[]{:S(2)}) copy-start(s32[256]{0:T(256)} %param.13) | copy-start | bytes 3076
  17.6 40.1 %all-to-all-start = ((bf16[32,32,512]{2,1,0:T(8,128)(2,1)}), bf16[32,32,512]{2,1,0:T(8,128)(2,1)S(1)}, u32[]{:S(2)}, u32[]{:S(2)}) async-start(bf16[32,32,512]{2,1,0:T(8,128)(2,1)} %broadcast_select_fusion), calls=%async_computation.1 | async-start | bytes 2097152 | tf_op jit(solution)/shard_map/all_to_all | solution.py:53
  29.1 91.5 %all-reduce.3.cloned.1.call-start = ((), (), s32[]{:S(2)}) async-start(), calls=%async_computation.4 | async-start | bytes 524288 | tf_op jit(solution)/shard_map/psum | solution.py:57
  29.3 7.1 %copy-start.2 = (bf16[8,512,64]{1,2,0:T(8,128)(2,1)S(1)}, bf16[8,512,64]{1,2,0:T(8,128)(2,1)}, u32[]{:S(2)}) copy-start(bf16[8,512,64]{1,2,0:T(8,128)(2,1)} %param.11) | copy-start | bytes 1572868
  38.4 22.5 %copy-start.3 = (bf16[512,512]{1,0:T(8,128)(2,1)S(1)}, bf16[512,512]{1,0:T(8,128)(2,1)}, u32[]{:S(2)}) copy-start(bf16[512,512]{1,0:T(8,128)(2,1)} %param.8) | copy-start | bytes 1572868
  60.8 132.4 %reduce-scatter.2.cloned.1.call-start = ((), (), s32[]{:S(2)}) async-start(), calls=%async_computation.3 | async-start | bytes 9437184 | tf_op jit(solution)/shard_map/reduce_scatter | solution.py:48
  125.1 60.5 %all-to-all-start.1 = ((bf16[32,32,1024]{2,1,0:T(8,128)(2,1)}), bf16[32,32,1024]{2,1,0:T(8,128)(2,1)S(1)}, u32[]{:S(2)}, u32[]{:S(2)}) async-start(bf16[32,32,1024]{2,1,0:T(8,128)(2,1)} %fusion.7), calls=%async_computation.2 | async-start | bytes 4194304 | tf_op jit(solution)/shard_map/all_to_all | solution.py:64
Sparse Core Ops, SparseCore 0:
  61.0 59.6 all-reduce.2
  123.2 54.4 reduce-scatter.1
where the time goes:
time: 204 us; the launch traced here: 203 us
  waiting for transfers between devices  117 us (57%)
  local copies, waits for them, and re-layouts  24.1 us (12%)
  starting transfers between devices  21.4 us (10%)
  matrix products  17.6 us (9%)
  between operations  13.6 us (7%)
  other arithmetic  9.67 us (5%)
    all_to_all x1, waiting for transfers between devices, per_device(): lax.all_to_all(raised_output.astype(jnp.bfloat16), 'req', split_axis=0, c...  50.4 us
    psum x1, waiting for transfers between devices, per_device(): lax.psum(reduced_rows.astype(jnp.bfloat16), 'tensor').astype(jnp.float32)  46.8 us
    all_to_all x1, waiting for transfers between devices, per_device(): lax.all_to_all(outgoing, 'req', split_axis=0, concat_axis=0, tiled=True)  19.3 us
    all_to_all x1, starting transfers between devices, per_device(): lax.all_to_all(outgoing, 'req', split_axis=0, concat_axis=0, tiled=True)  11.5 us
    dot_general x1, matrix products, per_device(): jnp.dot(attention_output, projection_weight, preferred_element_type=jnp.f...  10.1 us
    all_to_all x1, starting transfers between devices, per_device(): lax.all_to_all(raised_output.astype(jnp.bfloat16), 'req', split_axis=0, c...  9.85 us
    gather x2, local copies, waits for them, and re-layouts, per_device(): all_slots = jnp.take(adapter_pool_slot, request_adapter_id)  6.9 us
    gather x1, local copies, waits for them, and re-layouts, per_device(): jnp.take(flat, tok_owner * most_rows + positions - tok_start, axis=0)  5.01 us
  transfers between devices with their start and end apart: 4, of which 3 were waited for; matrix products, arithmetic and copies ran while one was open for 17% of the time, Pallas kernels for 0%

commit v1 on v0

--- a/solution.py
+++ b/solution.py
@@ -2,6 +2,11 @@
 import jax.numpy as jnp
 from jax import lax
 from jax.sharding import PartitionSpec as P
+
+
+def gather_and_add(array, name):
+    parts = lax.all_gather(array, name)
+    return jnp.sum(parts, axis=0)
 
 
 def per_device(
@@ -54,7 +59,7 @@
         selected_down_map,
         preferred_element_type=jnp.float32,
     )
-    reduced_rows = lax.psum(reduced_rows.astype(jnp.bfloat16), "tensor").astype(jnp.float32)
+    reduced_rows = gather_and_add(reduced_rows.astype(jnp.bfloat16), "tensor").astype(jnp.float32)
     raised_output = jnp.einsum(
         "iut,itb->iub",
         reduced_rows.astype(jnp.bfloat16),

time: 204 us -> 170 us (0.83)
  waiting for transfers between devices: 117 us -> 79.9 us
  other arithmetic: 9.67 us -> 11.8 us
    psum x1 -> x0, waiting for transfers between devices: 46.8 us -> none  [per_device(): lax.psum(reduced_rows.astype(jnp.bfloat16), 'tensor').astype(jnp.float32)]
    all_gather x0 -> x1, waiting for transfers between devices: none -> 10.3 us  [gather_and_add(): parts = lax.all_gather(array, name)]
    reduce_sum x0 -> x1, other arithmetic: none -> 2.1 us  [gather_and_add(): return jnp.sum(parts, axis=0)]
  transfers between devices with their start and end apart: 4 -> 4, of which waited for: 3 -> 3; matrix products, arithmetic and copies ran while one was open for 17% -> 22% of each run, Pallas kernels for 0% -> 0%
where the time goes in v1:
time: 170 us; the launch traced here: 168 us
  waiting for transfers between devices  79.9 us (47%)
  local copies, waits for them, and re-layouts  24.1 us (14%)
  starting transfers between devices  21.4 us (13%)
  matrix products  17.5 us (10%)
  between operations  13.6 us (8%)
  other arithmetic  11.8 us (7%)
    all_to_all x1, waiting for transfers between devices, per_device(): lax.all_to_all(raised_output.astype(jnp.bfloat16), 'req', split_axis=0, c...  50.1 us
    all_to_all x1, waiting for transfers between devices, per_device(): lax.all_to_all(outgoing, 'req', split_axis=0, concat_axis=0, tiled=True)  19.3 us
    all_to_all x1, starting transfers between devices, per_device(): lax.all_to_all(outgoing, 'req', split_axis=0, concat_axis=0, tiled=True)  11.5 us
    all_gather x1, waiting for transfers between devices, gather_and_add(): parts = lax.all_gather(array, name)  10.3 us
    dot_general x1, matrix products, per_device(): jnp.dot(attention_output, projection_weight, preferred_element_type=jnp.f...  10.1 us
    all_to_all x1, starting transfers between devices, per_device(): lax.all_to_all(raised_output.astype(jnp.bfloat16), 'req', split_axis=0, c...  9.85 us
    gather x2, local copies, waits for them, and re-layouts, per_device(): all_slots = jnp.take(adapter_pool_slot, request_adapter_id)  6.9 us
    gather x1, local copies, waits for them, and re-layouts, per_device(): jnp.take(flat, tok_owner * most_rows + positions - tok_start, axis=0)  5.01 us
  transfers between devices with their start and end apart: 4, of which 3 were waited for; matrix products, arithmetic and copies ran while one was open for 22% of the time, Pallas kernels for 0%

profile of v1, /device:TPU:6, one launch (start us, length us, event | category | flops | bytes accessed | tf_op | source)
XLA Modules:
  0.0 168.2 jit_solution(7750403156298052978)
XLA Ops:
  6.5 0.8 fusion.22
  7.3 0.7 copy.12
  8.2 1.4 gather_fusion
  9.6 0.7 fusion.24
  10.3 0.8 select_reduce_fusion.3
  11.4 1.1 concatenate.3
  12.5 4.0 %gather_fusion.1 = bf16[1024,512]{1,0:T(8,128)(2,1)S(1)} fusion(bf16[513,512]{1,0:T(8,128)(2,1)S(1)} %concatenate.3, s32[1024]{0:T(1024)S(1)} %broadcast_clamp_fusion), kind=kCustom, calls=%fused_computation.1 | custom fusion | bytes 2101248 | tf_op jit(solution)/shard_map/jit(_take)/gather | solution.py:51
  16.5 1.2 broadcast_select_fusion
  17.6 11.5 %all-to-all-start = ((bf16[32,32,512]{2,1,0:T(8,128)(2,1)}), bf16[32,32,512]{2,1,0:T(8,128)(2,1)S(1)}, u32[]{:S(2)}, u32[]{:S(2)}) async-start(bf16[32,32,512]{2,1,0:T(8,128)(2,1)} %broadcast_select_fusion), calls=%async_computation.1 | async-start | bytes 2097152 | tf_op jit(solution)/shard_map/all_to_all | solution.py:58
  29.3 6.8 %gather_fusion.2 = s32[1024]{0:T(1024)S(1)} fusion(s32[256]{0:T(256)S(1)} %copy-done.1, s32[1024]{0:T(1024)S(1)} %broadcast_clamp_fusion.1), kind=kCustom, calls=%fused_computation.2 | custom fusion | bytes 12288 | tf_op jit(solution)/shard_map/jit(_take)/gather | solution.py:38
  36.2 0.1 fusion.16
  36.4 2.0 %gather_fusion.3 = bf16[32,512,64]{1,2,0:T(8,128)(2,1)} fusion(bf16[8,512,64]{1,2,0:T(8,128)(2,1)S(1)} %copy-done.2, s32[1024]{0:T(1024)S(1)} %pad_clamp_fusion.1), kind=kCustom, calls=%fused_computation.3 | custom fusion | bytes 4194432 | tf_op jit(solution)/shard_map/jit(_take)/gather | solution.py:41
  38.4 19.3 %all-to-all-done = bf16[32,32,512]{2,1,0:T(8,128)(2,1)S(1)} async-done(((bf16[32,32,512]{2,1,0:T(8,128)(2,1)}), bf16[32,32,512]{2,1,0:T(8,128)(2,1)S(1)}, u32[]{:S(2)}, u32[]{:S(2)}) %all-to-all-start) | async-done | bytes 1048608 | tf_op jit(solution)/shard_map/all_to_all | solution.py:58
  57.7 3.1 %fusion.10 = bf16[32,32,64]{2,1,0:T(8,128)(2,1)} fusion(bf16[32,32,512]{2,1,0:T(8,128)(2,1)S(1)} %all-to-all-done, bf16[32,512,64]{1,2,0:T(8,128)(2,1)} %gather_fusion.3, pred[32]{0:T(512)(128)(4,1)S(1)} %compare_and_fusion), kind=kOutput, calls=%fused_computation.17 | convolution fusion | flops 68222976 | bytes 3276832 | tf_op jit(solution)/shard_map/sdy,syj->sdj/dot_general | solution.py:56
  60.9 10.1 %convolution_convert_fusion = bf16[512,8192]{1,0:T(8,128)(2,1)} fusion(bf16[512,512]{1,0:T(8,128)(2,1)S(1)} %copy-done.3, bf16[512,8192]{1,0:T(8,128)(2,1)} %param.10), kind=kOutput, calls=%fused_computation.6 | convolution fusion | flops 4299161600 | bytes 17301504 | tf_op jit(solution)/shard_map/dot_general | solution.py:52
  71.0 2.8 %gather_fusion.4 = bf16[32,64,1024]{2,1,0:T(8,128)(2,1)} fusion(bf16[8,64,1024]{2,1,0:T(8,128)(2,1)S(1)} %copy-done, s32[1024]{0:T(1024)S(1)} %pad_clamp_fusion.1), kind=kCustom, calls=%fused_computation.4 | custom fusion | bytes 8388736 | tf_op jit(solution)/shard_map/jit(_take)/gather | solution.py:42
  73.8 10.3 %all-gather.3.cloned.1.call-done = bf16[256,32,64]{2,1,0:T(8,128)(2,1)} async-done(((bf16[32,32,64]{2,1,0:T(8,128)(2,1)}), bf16[256,32,64]{2,1,0:T(8,128)(2,1)}) %all-gather.3.cloned.1.call-update) | async-done | bytes 1048592 | tf_op jit(solution)/shard_map/all_gather | solution.py:8
  84.1 2.1 %reduce_sum.77 = bf16[32,32,64]{2,1,0:T(8,128)(2,1)S(1)} reduce(bf16[8,32,32,64]{3,2,1,0:T(8,128)(2,1)} %bitcast.37, bf16[]{:T(256)} %constant.133.clone.1), dimensions={0}, to_apply=%region_8.9 | reduce | flops 458752 | bytes 1179650 | tf_op jit(solution)/shard_map/reduce_sum | solution.py:9
  86.2 4.3 %fusion.7 = bf16[32,32,1024]{2,1,0:T(8,128)(2,1)} fusion(bf16[32,32,64]{2,1,0:T(8,128)(2,1)S(1)} %reduce_sum.77, bf16[32,64,1024]{2,1,0:T(8,128)(2,1)} %gather_fusion.4, pred[32]{0:T(512)(128)(4,1)S(1)} %compare_and_fusion), kind=kOutput, calls=%fused_computation.16 | convolution fusion | flops 137363456 | bytes 6422560 | tf_op jit(solution)/shard_map/iut,itb->iub/dot_general | solution.py:63
  90.6 9.8 %all-to-all-start.1 = ((bf16[32,32,1024]{2,1,0:T(8,128)(2,1)}), bf16[32,32,1024]{2,1,0:T(8,128)(2,1)S(1)}, u32[]{:S(2)}, u32[]{:S(2)}) async-start(bf16[32,32,1024]{2,1,0:T(8,128)(2,1)} %fusion.7), calls=%async_computation.2 | async-start | bytes 4194304 | tf_op jit(solution)/shard_map/all_to_all | solution.py:69
  100.7 50.1 %all-to-all-done.1 = bf16[32,32,1024]{2,1,0:T(8,128)(2,1)S(1)} async-done(((bf16[32,32,1024]{2,1,0:T(8,128)(2,1)}), bf16[32,32,1024]{2,1,0:T(8,128)(2,1)S(1)}, u32[]{:S(2)}, u32[]{:S(2)}) %all-to-all-start.1) | async-done | bytes 2097184 | tf_op jit(solution)/shard_map/all_to_all | solution.py:69
  150.8 2.6 %bitcast_convert_fusion = f32[1024,1024]{1,0:T(8,128)} fusion(bf16[32,32,1024]{2,1,0:T(8,128)(2,1)S(1)} %all-to-all-done.1), kind=kLoop, calls=%fused_computation.10 | loop fusion | flops 1048576 | bytes 6291456 | tf_op jit(solution)/shard_map/reshape | solution.py:72
  153.4 5.0 %gather_fusion.5 = f32[512,1024]{1,0:T(8,128)S(1)} fusion(f32[1024,1024]{1,0:T(8,128)} %bitcast_convert_fusion, s32[1024]{0:T(1024)S(1)} %pad_clamp_fusion), kind=kCustom, calls=%fused_computation.5 | custom fusion | bytes 4196352 | tf_op jit(solution)/shard_map/jit(_take)/gather | solution.py:73
  158.4 2.9 %add_convert_fusion = bf16[512,1024]{1,0:T(8,128)(2,1)} fusion(f32[512,1024]{1,0:T(8,128)S(1)} %gather_fusion.5, bf16[512,1024]{1,0:T(8,128)(2,1)} %reduce-scatter.2.cloned.1.call-done, bf16[512,1024]{1,0:T(8,128)(2,1)} %param.9, pred[512]{0:T(512)(128)(4,1)S(1)} %compare_and_fusion.1), kind=kLoop, calls=%fused_computation.11 | loop fusion | flops 3145728 | bytes 5243392 | tf_op jit(solution)/shard_map/convert_element_type | solution.py:74
  (35 shorter events, 1.0 us)
Async XLA Ops:
  6.5 64.5 %copy-start = (bf16[8,64,1024]{2,1,0:T(8,128)(2,1)S(1)}, bf16[8,64,1024]{2,1,0:T(8,128)(2,1)}, u32[]{:S(2)}) copy-start(bf16[8,64,1024]{2,1,0:T(8,128)(2,1)} %param.12) | copy-start | bytes 3145732
  16.4 12.7 %copy-start.4 = (s32[32,32]{1,0:T(8,128)S(1)}, s32[32,32]{1,0:T(8,128)}, u32[]{:S(2)}) copy-start(s32[32,32]{1,0:T(8,128)} %param.14) | copy-start | bytes 12292
  16.4 12.8 %copy-start.1 = (s32[256]{0:T(256)S(1)}, s32[256]{0:T(256)}, u32[]{:S(2)}) copy-start(s32[256]{0:T(256)} %param.13) | copy-start | bytes 3076
  17.6 40.1 %all-to-all-start = ((bf16[32,32,512]{2,1,0:T(8,128)(2,1)}), bf16[32,32,512]{2,1,0:T(8,128)(2,1)S(1)}, u32[]{:S(2)}, u32[]{:S(2)}) async-start(bf16[32,32,512]{2,1,0:T(8,128)(2,1)} %broadcast_select_fusion), calls=%async_computation.1 | async-start | bytes 2097152 | tf_op jit(solution)/shard_map/all_to_all | solution.py:58
  29.1 55.0 %all-gather.3.cloned.1.call-start = ((), (), s32[]{:S(2)}) async-start(), calls=%async_computation.4 | async-start | bytes 2359296 | tf_op jit(solution)/shard_map/all_gather | solution.py:8
  29.3 7.1 %copy-start.2 = (bf16[8,512,64]{1,2,0:T(8,128)(2,1)S(1)}, bf16[8,512,64]{1,2,0:T(8,128)(2,1)}, u32[]{:S(2)}) copy-start(bf16[8,512,64]{1,2,0:T(8,128)(2,1)} %param.11) | copy-start | bytes 1572868
  38.4 22.5 %copy-start.3 = (bf16[512,512]{1,0:T(8,128)(2,1)S(1)}, bf16[512,512]{1,0:T(8,128)(2,1)}, u32[]{:S(2)}) copy-start(bf16[512,512]{1,0:T(8,128)(2,1)} %param.8) | copy-start | bytes 1572868
  60.8 97.6 %reduce-scatter.2.cloned.1.call-start = ((), (), s32[]{:S(2)}) async-start(), calls=%async_computation.3 | async-start | bytes 9437184 | tf_op jit(solution)/shard_map/reduce_scatter | solution.py:53
  90.6 60.2 %all-to-all-start.1 = ((bf16[32,32,1024]{2,1,0:T(8,128)(2,1)}), bf16[32,32,1024]{2,1,0:T(8,128)(2,1)S(1)}, u32[]{:S(2)}, u32[]{:S(2)}) async-start(bf16[32,32,1024]{2,1,0:T(8,128)(2,1)} %fusion.7), calls=%async_computation.2 | async-start | bytes 4194304 | tf_op jit(solution)/shard_map/all_to_all | solution.py:69
Sparse Core Ops, SparseCore 0:
  61.0 23.1 all-gather.2
  86.7 54.7 reduce-scatter.1
